TPU v7x, 32 devices: a whole 2x2x4 slice. The times are simulated.
32 devices in a mesh: rep: 4 (over y, core), dp: 8 (over z, x).
Axes of the slice: x: 2, y: 2, z: 4, core: 2. Of those that a mesh axis runs over, the one named last changes fastest.
Arguments:
- query_states: bfloat16 [256, 32, 768], P(('rep', 'dp')), may hold values from -12 to 12
- passage_states: bfloat16 [128, 180, 768], P(('rep', 'dp')), may hold values from -12 to 12
- query_lengths: int32 [256], P(('rep', 'dp')), may hold values from 8 to 32, as said below
- passage_lengths: int32 [128], P(('rep', 'dp')), may hold values from 45 to 180, as said below
- passage_ids: int32 [128, 180], P(('rep', 'dp')), may hold values from 2 to 30521, as said below
- positives: int32 [256], P(('rep', 'dp')), may hold values from 0 to 31, as said below
- up_weight: bfloat16 [768, 3072], replicated, may hold values from -0.21875 to 0.21875
- up_bias: float32 [3072], replicated, may hold values from -3 to 3
- down_weight: bfloat16 [3072, 768], replicated, may hold values from -0.109375 to 0.109375
- down_bias: float32 [768], replicated, may hold values from -3 to 3
- norm_gain: float32 [768], replicated, may hold values from 0.5 to 1.5
- norm_bias: float32 [768], replicated, may hold values from -2 to 2
- proj_weight: bfloat16 [768, 128], replicated, may hold values from -0.21875 to 0.21875
Outputs:
- mean_loss: float32 [], replicated
- passage_grad: float32 [128, 180, 128], P(('rep', 'dp'))
- proj_grad: float32 [768, 128], replicated
Inputs may be any that keep to these rules, and one draw needn't show every extreme that they name: `query_lengths`: every device holds a query with all 32 slots real. `passage_lengths`: every device holds a passage with all 180 slots real. `passage_ids`: slots 0 and 1 of every passage hold ids 101 and 2; ids 999 to 1066 are punctuation. `positives`: index of the positive passage among the 32 passages of the query's replica group, in the order of the devices.
All inputs are finite; a program needn't handle non-finite values.
Results may differ from a plain program's by a relative error of at most 0.0055.
Values may be sent and summed in bfloat16 or wider, within the bound.
A program may use at most 128 MiB of HBM per device.

v0:
```python
import math

import jax
import jax.numpy as jnp
from jax import lax
from jax.sharding import PartitionSpec as P

temper = 0.05
eps_norm = 1e-06
punct_low = 999
punct_high = 1067


def encode_rows(
    token_rows, up_weight, up_bias, down_weight, down_bias, norm_gain, norm_bias, proj_weight
):
    upward = jnp.dot(token_rows, up_weight, preferred_element_type=jnp.float32) + up_bias
    activated = jax.nn.gelu(upward, approximate=False).astype(jnp.bfloat16)
    residual = (
        token_rows.astype(jnp.float32)
        + jnp.dot(activated, down_weight, preferred_element_type=jnp.float32)
        + down_bias
    )
    average = jnp.mean(residual, -1, keepdims=True)
    centered = residual - average
    variance = jnp.mean(centered * centered, -1, keepdims=True)
    hidden = (centered * lax.rsqrt(variance + eps_norm) * norm_gain + norm_bias).astype(
        jnp.bfloat16
    )
    projected = jnp.dot(hidden, proj_weight, preferred_element_type=jnp.float32)
    inverse = lax.rsqrt(jnp.sum(projected * projected, -1, keepdims=True) + eps_norm)
    return (hidden, projected * inverse, inverse)


def token_scores(query_flat, query_keep, block_emb, block_keep, query_count):
    item_count, pass_len, embed_dim = block_emb.shape
    flat_block = block_emb.reshape(item_count * pass_len, embed_dim)
    similar = lax.dot_general(
        query_flat, flat_block, (((1,), (1,)), ((), ())), preferred_element_type=jnp.float32
    )
    weights = (
        jnp.exp(similar / temper).reshape(-1, item_count, pass_len)
        * block_keep.astype(jnp.float32)[None]
    )
    totals = jnp.sum(weights, -1)
    soft_max = temper * jnp.log(totals) * query_keep[:, None]
    scores = jnp.sum(soft_max.reshape(query_count, -1, item_count), 1)
    return (scores, weights, totals)


def token_grads(query_flat, query_keep, block_emb, weights, totals, dscore, query_count):
    item_count, pass_len, embed_dim = block_emb.shape
    factor = (dscore[:, None, :] * query_keep.reshape(query_count, -1)[:, :, None]).reshape(
        -1, item_count
    ) / totals
    sim_grad = (
        (weights * factor[:, :, None]).reshape(-1, item_count * pass_len).astype(jnp.bfloat16)
    )
    flat_block = block_emb.reshape(item_count * pass_len, embed_dim)
    passage_term = lax.dot_general(
        sim_grad, query_flat, (((0,), (0,)), ((), ())), preferred_element_type=jnp.float32
    )
    query_term = jnp.dot(sim_grad, flat_block, preferred_element_type=jnp.float32)
    return (passage_term.reshape(item_count, pass_len, embed_dim), query_term)


def cross_entropy(scores, positives):
    log_total = jnp.log(jnp.sum(jnp.exp(scores), 1))
    onehot = (jnp.arange(scores.shape[1], dtype=jnp.int32)[None, :] == positives[:, None]).astype(
        jnp.float32
    )
    loss_sum = jnp.sum(log_total - jnp.sum(scores * onehot, 1))
    dscore = jnp.exp(scores - log_total[:, None]) - onehot
    return (loss_sum, dscore)


def norm_backward(gradient, normed, inverse):
    return (inverse * (gradient - normed * jnp.sum(normed * gradient, -1, keepdims=True))).astype(
        jnp.bfloat16
    )


def per_device(
    query_states,
    passage_states,
    query_lengths,
    passage_lengths,
    passage_ids,
    positives,
    up_weight,
    up_bias,
    down_weight,
    down_bias,
    norm_gain,
    norm_bias,
    proj_weight,
):
    query_count, query_len, model_width = query_states.shape
    pass_count, pass_len, _ = passage_states.shape
    embed_dim = proj_weight.shape[1]
    token_rows = jnp.concatenate(
        [query_states.reshape(-1, model_width), passage_states.reshape(-1, model_width)], 0
    )
    hidden, normed, inverse = encode_rows(
        token_rows, up_weight, up_bias, down_weight, down_bias, norm_gain, norm_bias, proj_weight
    )
    boundary = query_count * query_len
    query_emb = normed[:boundary].astype(jnp.bfloat16)
    pass_emb = normed[boundary:].astype(jnp.bfloat16).reshape(pass_count, pass_len, embed_dim)
    query_keep = (
        (jnp.arange(query_len, dtype=jnp.int32)[None, :] < query_lengths[:, None])
        .astype(jnp.float32)
        .reshape(-1)
    )
    is_punct = (passage_ids >= punct_low) & (passage_ids < punct_high)
    pass_keep = (
        (jnp.arange(pass_len, dtype=jnp.int32)[None, :] < passage_lengths[:, None])
        & jnp.logical_not(is_punct)
    ).astype(jnp.bfloat16)
    groups = lax.axis_size("dp")
    gathered, gathered_keep = (
        lax.all_gather(pass_emb, "dp", axis=0, tiled=True),
        lax.all_gather(pass_keep, "dp", axis=0, tiled=True),
    )
    group_pass = pass_count * groups
    block_pass = math.gcd(group_pass, 16)
    block_count = group_pass // block_pass
    emb_blocks = gathered.reshape(block_count, block_pass, pass_len, embed_dim)
    keep_blocks = gathered_keep.reshape(block_count, block_pass, pass_len)

    def forward(paired):
        scores, _, _ = token_scores(query_emb, query_keep, paired[0], paired[1], query_count)
        return scores

    stacked = lax.map(forward, (emb_blocks, keep_blocks))
    scores = jnp.transpose(stacked, (1, 0, 2)).reshape(query_count, group_pass)
    loss_sum, dscore = cross_entropy(scores, positives)
    grad_blocks = jnp.transpose(dscore.reshape(query_count, block_count, block_pass), (1, 0, 2))

    def backward(query_grad, triple):
        block_emb, block_keep, block_grad = triple
        _, weights, totals = token_scores(query_emb, query_keep, block_emb, block_keep, query_count)
        passage_term, query_term = token_grads(
            query_emb, query_keep, block_emb, weights, totals, block_grad, query_count
        )
        return (query_grad + query_term, passage_term)

    start_grad = jnp.zeros((query_count * query_len, embed_dim), jnp.float32)
    query_grad, pass_terms = lax.scan(backward, start_grad, (emb_blocks, keep_blocks, grad_blocks))
    passage_grad = lax.psum_scatter(
        pass_terms.reshape(group_pass, pass_len, embed_dim), "dp", scatter_dimension=0, tiled=True
    )
    query_back = norm_backward(query_grad, normed[:boundary], inverse[:boundary])
    pass_back = norm_backward(
        passage_grad.reshape(-1, embed_dim), normed[boundary:], inverse[boundary:]
    )
    all_back = jnp.concatenate([query_back, pass_back], 0)
    local_sum = lax.dot_general(
        hidden, all_back, (((0,), (0,)), ((), ())), preferred_element_type=jnp.float32
    )
    proj_total, loss_total = lax.psum((local_sum, loss_sum), ("rep", "dp"))
    mean_loss = loss_total / (query_count * lax.axis_size("rep") * groups)
    return (mean_loss, passage_grad, proj_total)


def solution(mesh):
    in_specs = (
        P(("rep", "dp"), None, None),
        P(("rep", "dp"), None, None),
        P(("rep", "dp")),
        P(("rep", "dp")),
        P(("rep", "dp"), None),
        P(("rep", "dp")),
        P(),
        P(),
        P(),
        P(),
        P(),
        P(),
        P(),
    )
    out_specs = (P(), P(("rep", "dp"), None, None), P())
    return jax.shard_map(
        per_device, mesh=mesh, in_specs=in_specs, out_specs=out_specs, check_vma=False
    )
```

profile of v0, /device:TPU:0, one launch (start us, length us, event | category | flops | bytes accessed | tf_op | source)
XLA Modules:
  0.0 375.2 jit_solution(12768285296816217812)
XLA Ops:
  7.2 1.4 copy.29
  9.8 39.0 %fusion.77 = (f32[976]{0:T(1024)S(1)}, f32[976,768]{1,0:T(8,128)S(1)}) fusion(f32[768]{0:T(1024)} %param.26, bf16[3072,768]{1,0:T(8,128)(2,1)} %param.25, f32[3072]{0:T(1024)} %param.24, bf16[768,3072]{1,0:T(8,128)(2,1)} %param.23, bf16[720,768]{1,0:T(8,128)(2,1)} %reshape.166, bf16[256,768]{1,0:T(8,128)(2,1)} %bitcast.86), kind=kOutput, calls=%fused_computation.113 | convolution fusion | flops 9416821760 | bytes 13953856 | tf_op jit(solution)/shard_map/dot_general | solution.py:21
  53.0 27.9 %all-gather = bf16[8,4,180]{2,1,0:T(4,128)(2,1)S(1)} all-gather(bf16[1,4,180]{2,1,0:T(4,128)(2,1)S(1)} %fusion.42), channel_id=1, replica_groups=mesh['rep'=4,'dp'=8] {'dp'}, dimensions={0}, use_global_device_ids=true | all-gather | bytes 12960 | tf_op jit(solution)/shard_map/all_gather | solution.py:123
  80.9 18.3 %all-gather.3.cloned.1.call-done = bf16[32,180,128]{2,1,0:T(8,128)(2,1)} async-done(((bf16[4,180,128]{2,1,0:T(8,128)(2,1)}), bf16[32,180,128]{2,1,0:T(8,128)(2,1)}) %all-gather.3.cloned.1.call-update) | async-done | bytes 1474576 | tf_op jit(solution)/shard_map/all_gather | solution.py:122
  99.3 13.9 %while.24 = (s32[]{:T(128)}, f32[2,8,16]{2,1,0:T(8,128)S(1)}, bf16[2,16,180,128]{3,2,1,0:T(8,128)(2,1)}, bf16[256,128]{1,0:T(8,128)(2,1)S(1)}, bf16[2,16,180]{2,1,0:T(8,128)(2,1)S(1)}, /*index=5*/s32[8]{0:T(128)S(1)}, s32[]{:T(128)}) while((s32[]{:T(128)}, f32[2,8,16]{2,1,0:T(8,128)S(1)}, bf16[2,16,180,128]{3,2,1,0:T(8,128)(2,1)}, ...), condition=%wide.region_6.7_spmd.clone, body=%wide.region_3.6_spmd.clone.sunk | while | flops 190962880 | bytes 15687425 | solution.py:135
  100.7 2.2 fusion.106
  102.9 2.6 reshape.189
  107.6 2.2 fusion.106
  109.8 2.6 reshape.189
  114.1 45.3 %while.25 = (s32[]{:T(128)}, f32[256,128]{1,0:T(8,128)S(1)}, f32[2,16,180,128]{3,2,1,0:T(8,128)}, bf16[2,16,180,128]{3,2,1,0:T(8,128)(2,1)}, bf16[256,128]{1,0:T...) while((s32[]{:T(128)}, f32[256,128]{1,0:T(8,128)S(1)}, ...), condition=%wide.region_13.14_spmd.clone, body=%wide.region_11.13_spmd.clone.sunk | while | flops 570727744 | bytes 49299292 | solution.py:149
  114.6 1.2 constant_dynamic-slice_fusion.5
  116.8 1.7 fusion.114
  118.5 1.8 reshape.191
  120.3 2.3 multiply_reduce_fusion.12
  122.7 1.9 mul.316
  124.5 4.1 %mul.317 = f32[256,2880]{0,1:T(8,128)} reshape(f32[256,16,180]{0,2,1:T(8,128)} %mul.316) | data formatting | bytes 5898240 | tf_op jit(solution)/shard_map/while/body/eval_jaxpr/mul | solution.py:57
  128.7 2.3 multiply_convert_fusion.4
  132.8 2.3 reshape.192
  135.1 1.7 bitcast_dynamic-update-slice_fusion.5
  139.5 1.7 fusion.114
  141.2 1.8 reshape.191
  143.0 2.3 multiply_reduce_fusion.12
  145.3 1.9 mul.316
  147.2 4.1 %mul.317 = f32[256,2880]{0,1:T(8,128)} reshape(f32[256,16,180]{0,2,1:T(8,128)} %mul.316) | data formatting | bytes 5898240 | tf_op jit(solution)/shard_map/while/body/eval_jaxpr/mul | solution.py:57
  151.3 2.3 multiply_convert_fusion.4
  155.5 2.3 reshape.192
  157.7 1.7 bitcast_dynamic-update-slice_fusion.5
  161.7 70.0 %reduce-scatter.2.cloned.1.call-done = f32[4,180,128]{2,1,0:T(8,128)} async-done(((f32[32,180,128]{2,1,0:T(8,128)}), f32[4,180,128]{2,1,0:T(8,128)}) %reduce-scatter.2.cloned.1.call-update) | async-done | bytes 368656 | tf_op jit(solution)/shard_map/reduce_scatter | solution.py:150
  234.2 1.4 fusion.34
  235.6 39.9 %psum.14 = f32[]{:T(128)} all-reduce(f32[]{:T(128)} %get-tuple-element.165), channel_id=1, replica_groups=mesh['rep'=4,'dp'=8] {'rep','dp'}, use_global_device_ids=true, to_apply=%region_10.11 | all-reduce | flops 1 | bytes 8 | tf_op jit(solution)/shard_map/psum | solution.py:161
  277.0 88.8 %all-reduce.2.cloned.1.call-done = f32[768,128]{1,0:T(8,128)} async-done(((f32[768,128]{1,0:T(8,128)}), f32[768,128]{1,0:T(8,128)}) %all-reduce.2.cloned.1.call-update) | async-done | bytes 393232 | tf_op jit(solution)/shard_map/psum | solution.py:161
  365.8 1.8 copy.53
  (109 shorter events, 23.7 us)
Async XLA Ops:
  7.2 43.8 %copy-start = (bf16[768,128]{1,0:T(8,128)(2,1)S(1)}, bf16[768,128]{1,0:T(8,128)(2,1)}, u32[]{:S(2)}) copy-start(bf16[768,128]{1,0:T(8,128)(2,1)} %param.29) | copy-start | bytes 589828
  7.2 92.1 %all-gather.3.cloned.1.call-start = ((), (), s32[]{:S(2)}) async-start(), calls=%async_computation.1 | async-start | bytes 1695744 | tf_op jit(solution)/shard_map/all_gather | solution.py:122
  9.7 39.6 %copy-start.10 = (f32[768]{0:T(1024)S(1)}, f32[768]{0:T(1024)}, u32[]{:S(2)}) copy-start(f32[768]{0:T(1024)} %param.28) | copy-start | bytes 9220
  9.8 39.6 %copy-start.11 = (f32[768]{0:T(1024)S(1)}, f32[768]{0:T(1024)}, u32[]{:S(2)}) copy-start(f32[768]{0:T(1024)} %param.27) | copy-start | bytes 9220
  49.3 3.6 copy-start.9
  49.3 3.6 copy-start.13
  49.3 50.0 %copy-start.8 = (s32[8]{0:T(128)S(1)}, s32[8]{0:T(128)}, u32[]{:S(2)}) copy-start(s32[8]{0:T(128)} %param.19) | copy-start | bytes 100
  49.9 1.1 copy-start.3
  51.9 47.4 %copy-start.5 = (f32[976,128]{1,0:T(8,128)}, f32[976,128]{1,0:T(8,128)S(1)}, u32[]{:S(2)}) copy-start(f32[976,128]{1,0:T(8,128)S(1)} %broadcast_multiply_fusion) | copy-start | bytes 1499140
  52.8 178.9 %reduce-scatter.2.cloned.1.call-start = ((), (), s32[]{:S(2)}) async-start(), calls=%async_computation.2 | async-start | bytes 3391488 | tf_op jit(solution)/shard_map/reduce_scatter | solution.py:150
  99.3 13.9 %copy-start.12 = (s32[8]{0:T(128)S(1)}, s32[8]{0:T(128)}, u32[]{:S(2)}) copy-start(s32[8]{0:T(128)} %param.22) | copy-start | bytes 100
  128.7 3.5 copy-start.2
  131.0 1.1 copy-start.1
  151.3 3.5 copy-start.2
  153.7 1.1 copy-start.1
  159.4 74.5 %copy-start.6 = (f32[976,128]{1,0:T(8,128)S(1)}, f32[976,128]{1,0:T(8,128)}, u32[]{:S(2)}) copy-start(f32[976,128]{1,0:T(8,128)} %copy-done.5) | copy-start | bytes 1499140
  159.4 74.8 %copy-start.4 = (bf16[976,768]{1,0:T(8,128)(2,1)S(1)}, bf16[976,768]{1,0:T(8,128)(2,1)}, u32[]{:S(2)}) copy-start(bf16[976,768]{1,0:T(8,128)(2,1)} %copy-done.3) | copy-start | bytes 4497412
  159.4 206.4 %all-reduce.2.cloned.1.call-start = ((), (), s32[]{:S(2)}) async-start(), calls=%async_computation.3 | async-start | bytes 786432 | tf_op jit(solution)/shard_map/psum | solution.py:161
  231.7 44.5 %copy-start.7 = (f32[4,180,128]{2,1,0:T(8,128)S(1)}, f32[4,180,128]{2,1,0:T(8,128)}, u32[]{:S(2)}) copy-start(f32[4,180,128]{2,1,0:T(8,128)} %reduce-scatter.2.cloned.1.call-done) | copy-start | bytes 1105924
Sparse Core Ops, SparseCore 0:
  52.9 46.3 all-gather.2
  159.6 72.0 reduce-scatter.1
  237.6 128.1 all-reduce.1
where the time goes:
time: 376 us; the launch traced here: 375 us
  waiting for transfers between devices  177 us (47%)
  blocking collectives  67.8 us (18%)
  matrix products  53.4 us (14%)
  local copies, waits for them, and re-layouts  44.1 us (12%)
  other arithmetic  16.6 us (4%)
  between operations  15.8 us (4%)
    psum x1, waiting for transfers between devices, per_device(): proj_total, loss_total = lax.psum((local_sum, loss_sum), ('rep', 'dp'))  88.8 us
    reduce_scatter x1, waiting for transfers between devices, per_device(): lax.psum_scatter(pass_terms.reshape(group_pass, pass_len, embed_dim), 'dp...  70 us
    psum x1, blocking collectives, per_device(): proj_total, loss_total = lax.psum((local_sum, loss_sum), ('rep', 'dp'))  39.9 us
    dot_general x1, matrix products, encode_rows(): jnp.dot(activated, down_weight, preferred_element_type=jnp.float32)  39 us
    all_gather x1, blocking collectives, per_device(): lax.all_gather(pass_keep, 'dp', axis=0, tiled=True)  27.9 us
    all_gather x1, waiting for transfers between devices, per_device(): lax.all_gather(pass_emb, 'dp', axis=0, tiled=True)  18.3 us
    mul x4, local copies, waits for them, and re-layouts, token_grads(): weights * factor[:, :, None]  12 us
    reshape x4, local copies, waits for them, and re-layouts, token_scores(): jnp.exp(similar / temper).reshape(-1, item_count, pass_len)  8.91 us
  transfers between devices with their start and end apart: 3, of which 3 were waited for; matrix products, arithmetic and copies ran while one was open for 1% of the time, Pallas kernels for 0%

commit v1 on v0

v1 whole, which is shorter than its diff:
```python
import functools

import jax
import jax.numpy as jnp
from jax import lax
from jax.experimental import pallas as pl
from jax.experimental.pallas import tpu as pltpu
from jax.sharding import PartitionSpec as P

MESH = pl.DeviceIdType.MESH

temper = 0.05
eps_norm = 1e-06
punct_low = 999
punct_high = 1067


def encode_rows(
    token_rows, up_weight, up_bias, down_weight, down_bias, norm_gain, norm_bias, proj_weight
):
    upward = jnp.dot(token_rows, up_weight, preferred_element_type=jnp.float32) + up_bias
    activated = jax.nn.gelu(upward, approximate=False).astype(jnp.bfloat16)
    residual = (
        token_rows.astype(jnp.float32)
        + jnp.dot(activated, down_weight, preferred_element_type=jnp.float32)
        + down_bias
    )
    average = jnp.mean(residual, -1, keepdims=True)
    centered = residual - average
    variance = jnp.mean(centered * centered, -1, keepdims=True)
    hidden = (centered * lax.rsqrt(variance + eps_norm) * norm_gain + norm_bias).astype(
        jnp.bfloat16
    )
    projected = jnp.dot(hidden, proj_weight, preferred_element_type=jnp.float32)
    inverse = lax.rsqrt(jnp.sum(projected * projected, -1, keepdims=True) + eps_norm)
    return (hidden, projected * inverse, inverse)


def greet(axes):
    barrier = pltpu.get_barrier_semaphore()
    count = 0
    for axis in axes:
        size = lax.axis_size(axis)
        me = lax.axis_index(axis)
        for off in range(1, size):
            pl.semaphore_signal(
                barrier, inc=1, device_id={axis: lax.rem(me + off, size)}, device_id_type=MESH
            )
        count += size - 1
    pl.semaphore_wait(barrier, count)


def send_all(axis, source, target, send_sem, recv_sem):
    size = lax.axis_size(axis)
    me = lax.axis_index(axis)
    copies = []
    for off in range(1, size):
        peer = lax.rem(me + off, size)
        copy = pltpu.make_async_remote_copy(
            src_ref=source(peer),
            dst_ref=target.at[me],
            send_sem=send_sem.at[off - 1],
            recv_sem=recv_sem.at[off - 1],
            device_id={axis: peer},
            device_id_type=MESH,
        )
        copy.start()
        copies.append(copy)
    return copies


def gather_kernel(*refs):
    count = len(refs) // 4
    sources, targets = refs[:count], refs[count : 2 * count]
    sems = refs[2 * count :]
    greet(("dp",))
    me = lax.axis_index("dp")
    copies = []
    for k in range(count):
        copies += send_all(
            "dp", lambda peer: sources[k], targets[k], sems[2 * k], sems[2 * k + 1]
        )
    for k in range(count):
        targets[k][me] = sources[k][...]
    for copy in copies:
        copy.wait()


def comm_params(collective_id):
    return pltpu.CompilerParams(collective_id=collective_id, has_side_effects=True)


def gather_dp(arrays, collective_id):
    size = lax.axis_size("dp")
    vmem = pl.BlockSpec(memory_space=pltpu.VMEM)
    return pl.pallas_call(
        gather_kernel,
        out_shape=[jax.ShapeDtypeStruct((size,) + a.shape, a.dtype) for a in arrays],
        in_specs=[vmem] * len(arrays),
        out_specs=[vmem] * len(arrays),
        scratch_shapes=[pltpu.SemaphoreType.DMA((size - 1,))] * (2 * len(arrays)),
        compiler_params=comm_params(collective_id),
    )(*arrays)


def scatter_kernel(parts, out, landed, send_sem, recv_sem):
    greet(("dp",))
    me = lax.axis_index("dp")
    copies = send_all("dp", lambda peer: parts.at[peer], landed, send_sem, recv_sem)
    landed[me] = parts[me]
    for copy in copies:
        copy.wait()
    total = landed[0].astype(jnp.float32)
    for k in range(1, lax.axis_size("dp")):
        total = total + landed[k].astype(jnp.float32)
    out[...] = total


def scatter_dp(parts, collective_id):
    size = lax.axis_size("dp")
    vmem = pl.BlockSpec(memory_space=pltpu.VMEM)
    return pl.pallas_call(
        scatter_kernel,
        out_shape=jax.ShapeDtypeStruct(parts.shape[1:], jnp.float32),
        in_specs=[vmem],
        out_specs=vmem,
        scratch_shapes=[pltpu.VMEM(parts.shape, parts.dtype)]
        + [pltpu.SemaphoreType.DMA((size - 1,))] * 2,
        compiler_params=comm_params(collective_id),
    )(parts)


def reduce_kernel(
    parts, loss, out, loss_out, landed, crossed, summed, full, s1, r1, s2, r2, s3, r3
):
    greet(("dp", "rep"))
    me = lax.axis_index("dp")
    mine = lax.axis_index("rep")
    rows = parts.shape[1]
    copies = send_all("dp", lambda peer: parts.at[peer], landed, s1, r1)
    landed[me] = parts[me]
    for copy in copies:
        copy.wait()
    total = landed[0].astype(jnp.float32)
    for k in range(1, lax.axis_size("dp")):
        total = total + landed[k].astype(jnp.float32)
    summed[0:rows] = total
    summed[rows:] = loss[...]
    copies = send_all("rep", lambda peer: summed, crossed, s2, r2)
    crossed[mine] = summed[...]
    for copy in copies:
        copy.wait()
    total = crossed[0]
    for k in range(1, lax.axis_size("rep")):
        total = total + crossed[k]
    loss_out[...] = total[rows:]
    full[me] = total[0:rows].astype(full.dtype)
    copies = send_all("dp", lambda peer: full.at[me], full, s3, r3)
    for copy in copies:
        copy.wait()
    out[...] = full[...].astype(jnp.float32)


def reduce_all(parts, loss, collective_id):
    size, reps = lax.axis_size("dp"), lax.axis_size("rep")
    rows, lanes = parts.shape[1:]
    vmem = pl.BlockSpec(memory_space=pltpu.VMEM)
    extra = loss.shape[0]
    return pl.pallas_call(
        reduce_kernel,
        out_shape=[
            jax.ShapeDtypeStruct(parts.shape, jnp.float32),
            jax.ShapeDtypeStruct(loss.shape, jnp.float32),
        ],
        in_specs=[vmem] * 2,
        out_specs=[vmem] * 2,
        scratch_shapes=[
            pltpu.VMEM(parts.shape, parts.dtype),
            pltpu.VMEM((reps, rows + extra, lanes), jnp.float32),
            pltpu.VMEM((rows + extra, lanes), jnp.float32),
            pltpu.VMEM(parts.shape, parts.dtype),
        ]
        + [pltpu.SemaphoreType.DMA((size - 1,))] * 2
        + [pltpu.SemaphoreType.DMA((reps - 1,))] * 2
        + [pltpu.SemaphoreType.DMA((size - 1,))] * 2,
        compiler_params=comm_params(collective_id),
    )(parts, loss)


def norm_backward(gradient, normed, inverse):
    return (inverse * (gradient - normed * jnp.sum(normed * gradient, -1, keepdims=True))).astype(
        jnp.bfloat16
    )


def tile_rows(array):
    return jnp.pad(array, ((0, -array.shape[0] % 8), (0, -array.shape[1] % 128)))


def per_device(
    query_states,
    passage_states,
    query_lengths,
    passage_lengths,
    passage_ids,
    positives,
    up_weight,
    up_bias,
    down_weight,
    down_bias,
    norm_gain,
    norm_bias,
    proj_weight,
):
    query_count, query_len, model_width = query_states.shape
    pass_count, pass_len, _ = passage_states.shape
    embed_dim = proj_weight.shape[1]
    groups = lax.axis_size("dp")
    token_rows = jnp.concatenate(
        [query_states.reshape(-1, model_width), passage_states.reshape(-1, model_width)], 0
    )
    hidden, normed, inverse = encode_rows(
        token_rows, up_weight, up_bias, down_weight, down_bias, norm_gain, norm_bias, proj_weight
    )
    boundary = query_count * query_len
    query_emb = normed[:boundary].astype(jnp.bfloat16)
    pass_emb = normed[boundary:].astype(jnp.bfloat16).reshape(pass_count, pass_len, embed_dim)
    is_punct = (passage_ids >= punct_low) & (passage_ids < punct_high)
    pass_keep = (
        (jnp.arange(pass_len, dtype=jnp.int32)[None, :] < passage_lengths[:, None])
        & jnp.logical_not(is_punct)
    ).astype(jnp.float32)

    facts = tile_rows(jnp.stack([query_lengths, positives]))
    all_emb, all_facts = gather_dp((query_emb, facts), 1)
    all_emb = all_emb.reshape(-1, embed_dim)
    all_lengths = all_facts[:, 0, :query_count].reshape(-1)
    all_positives = all_facts[:, 1, :query_count].reshape(-1)
    group_count = query_count * groups
    query_keep = (
        jnp.arange(query_len, dtype=jnp.int32)[None, :] < all_lengths[:, None]
    ).astype(jnp.float32)

    weights, totals = [], []
    for p in range(pass_count):
        similar = lax.dot_general(
            all_emb, pass_emb[p], (((1,), (1,)), ((), ())), preferred_element_type=jnp.float32
        )
        weight = jnp.exp(similar / temper) * pass_keep[p][None]
        weights.append(weight)
        totals.append(jnp.sum(weight, -1).reshape(group_count, query_len))
    scores = jnp.stack(
        [jnp.sum(temper * jnp.log(total) * query_keep, 1) for total in totals], 1
    )
    first = lax.axis_index("dp") * pass_count
    onehot = (
        first + jnp.arange(pass_count, dtype=jnp.int32)[None, :] == all_positives[:, None]
    ).astype(jnp.float32)
    shares = tile_rows(jnp.stack([jnp.sum(jnp.exp(scores), 1), jnp.sum(scores * onehot, 1)]))
    (all_shares,) = gather_dp((shares,), 2)
    both = jnp.sum(all_shares, 0)
    log_total = jnp.log(both[0, :group_count])
    loss_sum = jnp.sum(log_total - both[1, :group_count])
    dscore = jnp.exp(scores - log_total[:, None]) - onehot

    pass_terms = []
    query_part = None
    for p in range(pass_count):
        factor = (dscore[:, p : p + 1] * query_keep / totals[p]).reshape(-1, 1)
        sim_grad = (weights[p] * factor).astype(jnp.bfloat16)
        pass_terms.append(
            lax.dot_general(
                sim_grad, all_emb, (((0,), (0,)), ((), ())), preferred_element_type=jnp.float32
            )
        )
        term = jnp.dot(sim_grad, pass_emb[p], preferred_element_type=jnp.float32)
        query_part = term if query_part is None else query_part + term
    passage_grad = jnp.stack(pass_terms)
    query_grad = scatter_dp(
        query_part.astype(jnp.bfloat16).reshape(groups, boundary, embed_dim), 3
    )
    query_back = norm_backward(query_grad, normed[:boundary], inverse[:boundary])
    pass_back = norm_backward(
        passage_grad.reshape(-1, embed_dim), normed[boundary:], inverse[boundary:]
    )
    all_back = jnp.concatenate([query_back, pass_back], 0)
    local_sum = lax.dot_general(
        hidden, all_back, (((0,), (0,)), ((), ())), preferred_element_type=jnp.float32
    )
    proj_total, loss_total = reduce_all(
        local_sum.astype(jnp.bfloat16).reshape(groups, -1, embed_dim),
        jnp.full((8, 128), loss_sum, jnp.float32),
        4,
    )
    mean_loss = loss_total[0, 0] / (group_count * lax.axis_size("rep"))
    return (mean_loss, passage_grad, proj_total.reshape(model_width, embed_dim))


def solution(mesh):
    in_specs = (
        P(("rep", "dp"), None, None),
        P(("rep", "dp"), None, None),
        P(("rep", "dp")),
        P(("rep", "dp")),
        P(("rep", "dp"), None),
        P(("rep", "dp")),
        P(),
        P(),
        P(),
        P(),
        P(),
        P(),
        P(),
    )
    out_specs = (P(), P(("rep", "dp"), None, None), P())
    return jax.shard_map(
        per_device, mesh=mesh, in_specs=in_specs, out_specs=out_specs, check_vma=False
    )
```

time: 376 us -> 142 us (0.38)
  waiting for transfers between devices: 177 us -> 0 us
  blocking collectives: 67.8 us -> 0 us
  Pallas kernels: 0 us -> 62.9 us
  local copies, waits for them, and re-layouts: 44.1 us -> 11.6 us
  between operations: 15.8 us -> 2.76 us
  other arithmetic: 16.6 us -> 7.73 us
    psum x1 -> x0, waiting for transfers between devices: 88.8 us -> none  [per_device(): proj_total, loss_total = lax.psum((local_sum, loss_sum), ('rep', 'dp'))]
    reduce_scatter x1 -> x0, waiting for transfers between devices: 70 us -> none  [per_device(): lax.psum_scatter(pass_terms.reshape(group_pass, pass_len, embed_dim), 'dp...]
    pallas_call x0 -> x4, Pallas kernels: none -> 62.9 us  [the longest x2 28.5 us: gather_dp(): pl.pallas_call(gather_kernel, out_shape=[jax.ShapeDtypeStruct((size,) + a...]
    psum x1 -> x0, blocking collectives: 39.9 us -> none  [per_device(): proj_total, loss_total = lax.psum((local_sum, loss_sum), ('rep', 'dp'))]
    all_gather x1 -> x0, blocking collectives: 27.9 us -> none  [per_device(): lax.all_gather(pass_keep, 'dp', axis=0, tiled=True)]
    all_gather x1 -> x0, waiting for transfers between devices: 18.3 us -> none  [per_device(): lax.all_gather(pass_emb, 'dp', axis=0, tiled=True)]
    mul x16 -> x9, local copies, waits for them, and re-layouts: 12.8 us -> 0.59 us  [the longest x5 0.3 us: per_device(): factor = (dscore[:, p:p + 1] * query_keep / totals[p]).reshape(-1, 1)]
    reshape x10 -> x0, local copies, waits for them, and re-layouts: 12.1 us -> none  [the longest x4 8.91 us: token_scores(): jnp.exp(similar / temper).reshape(-1, item_count, pass_len)]
  transfers between devices with their start and end apart: 3 -> 0, of which waited for: 3 -> 0; matrix products, arithmetic and copies ran while one was open for 1% -> 0% of each run, Pallas kernels for 0% -> 0%
where the time goes in v1:
time: 142 us; the launch traced here: 141 us
  Pallas kernels  62.9 us (44%)
  matrix products  55.9 us (39%)
  local copies, waits for them, and re-layouts  11.6 us (8%)
  other arithmetic  7.73 us (5%)
  between operations  2.76 us (2%)
    dot_general x1, matrix products, encode_rows(): jnp.dot(activated, down_weight, preferred_element_type=jnp.float32)  39 us
    pallas_call x2, Pallas kernels, gather_dp(): pl.pallas_call(gather_kernel, out_shape=[jax.ShapeDtypeStruct((size,) + a...  28.5 us
    pallas_call x1, Pallas kernels, reduce_all(): pl.pallas_call(reduce_kernel, out_shape=[jax.ShapeDtypeStruct(parts.shape...  21.2 us
    pallas_call x1, Pallas kernels, scatter_dp(): pl.pallas_call(scatter_kernel, out_shape=jax.ShapeDtypeStruct(parts.shape...  13.2 us
    dot_general x4, matrix products, per_device(): lax.dot_general(all_emb, pass_emb[p], (((1,), (1,)), ((), ())), preferred...  7.64 us
    unnamed x27, local copies, waits for them, and re-layouts  5.12 us
    dot_general x4, matrix products, per_device(): lax.dot_general(sim_grad, all_emb, (((0,), (0,)), ((), ())), preferred_el...  4.4 us
    dot_general x4, matrix products, per_device(): term = jnp.dot(sim_grad, pass_emb[p], preferred_element_type=jnp.float32)  2.89 us

profile of v1, /device:TPU:0, one launch (start us, length us, event | category | flops | bytes accessed | tf_op | source)
XLA Modules:
  0.0 140.8 jit_solution(13738000910484093498)
XLA Ops:
  0.7 0.7 pad_add_fusion
  1.4 0.6 pad.8.refs_1_
  2.0 0.8 fusion.48
  2.8 1.4 copy.18
  4.1 1.1 reshape.202
  5.3 39.0 %fusion.86 = (f32[976]{0:T(1024)S(1)}, f32[976,768]{1,0:T(8,128)S(1)}) fusion(f32[768]{0:T(1024)S(1)} %copy-done.11, bf16[3072,768]{1,0:T(8,128)(2,1)} %param.21, f32[3072]{0:T(1024)S(1)} %copy-done.10, bf16[768,3072]{1,0:T(8,128)(2,1)} %param.19, bf16[720,768]{1,0:T(8,128)(2,1)} %reshape.202, bf16[256,768]{1,0:T(8,128)(2,1)} %bitcast.82), kind=kOutput, calls=%fused_computation.145 | convolution fusion | flops 9416821760 | bytes 13953856 | tf_op jit(solution)/shard_map/dot_general | solution.py:25
  45.0 0.5 add_convert_fusion
  45.5 0.6 multiply_reduce_fusion.1
  46.9 0.6 slice.139.refs_0_
  47.6 20.7 %shard_map.148 = (bf16[8,256,128]{2,1,0:T(8,128)(2,1)}, s32[8,8,128]{2,1,0:T(8,128)}) custom-call(bf16[256,128]{1,0:T(8,128)(2,1)} %slice.139.refs_0_, s32[8,128]{1,0:T(8,128)} %pad.8.refs_1_), custom_call_target="tpu_custom_call" | custom-call | tf_op jit(solution)/shard_map/pallas_call | solution.py:96
  68.3 0.9 slice_reduce_fusion.1
  69.3 2.7 %fusion.90 = (f32[2048]{0:T(1024)S(1)}, f32[2048,180]{0,1:T(8,128)}) fusion(f32[180]{0:T(256)S(1)} %bitcast.77, bf16[2048,128]{1,0:T(8,128)(2,1)} %bitcast.55, bf16[720,128]{1,0:T(8,128)(2,1)S(1)} %slice.138), kind=kOutput, calls=%fused_computation.147 | convolution fusion | flops 95475712 | bytes 2055168 | tf_op jit(solution)/shard_map/dot_general | solution.py:246
  72.1 2.7 %fusion.91 = (f32[2048]{0:T(1024)S(1)}, f32[2048,180]{0,1:T(8,128)}) fusion(f32[180]{0:T(256)S(1)} %bitcast.76, bf16[2048,128]{1,0:T(8,128)(2,1)} %bitcast.56, bf16[720,128]{1,0:T(8,128)(2,1)S(1)} %slice.138), kind=kOutput, calls=%fused_computation.148 | convolution fusion | flops 95475712 | bytes 2055168 | tf_op jit(solution)/shard_map/dot_general | solution.py:246
  74.9 1.7 %fusion.92 = (f32[2048]{0:T(1024)S(1)}, f32[2048,180]{0,1:T(8,128)}) fusion(f32[180]{0:T(256)S(1)} %bitcast.75, bf16[2048,128]{1,0:T(8,128)(2,1)S(1)} %bitcast.57, bf16[720,128]{1,0:T(8,128)(2,1)S(1)} %slice.138), kind=kOutput, calls=%fused_computation.149 | convolution fusion | flops 95475712 | bytes 2055168 | tf_op jit(solution)/shard_map/dot_general | solution.py:246
  76.6 0.5 fusion.89
  77.6 0.6 select_maximum_fusion.refs_0_
  78.2 7.8 %shard_map.149 = f32[8,8,128]{2,1,0:T(8,128)} custom-call(f32[8,128]{1,0:T(8,128)} %select_maximum_fusion.refs_0_), custom_call_target="tpu_custom_call" | custom-call | tf_op jit(solution)/shard_map/pallas_call | solution.py:96
  86.0 0.8 reduce_sum.166
  86.8 0.6 fusion.51
  87.5 1.2 broadcast_in_dim.2.loss
  89.2 1.9 %convolution_bitcast_fusion.2 = f32[1,180,128]{2,1,0:T(8,128)S(1)} fusion(bf16[2048,128]{1,0:T(8,128)(2,1)S(1)} %bitcast.59, f32[2048,180]{0,1:T(8,128)} %get-tuple-element.48, f32[2048]{0:T(1024)S(1)} %div.58), kind=kOutput, calls=%fused_computation.50 | convolution fusion | flops 95109120 | bytes 2099200 | tf_op jit(solution)/shard_map/dot_general | solution.py:272
  91.1 1.8 %convolution_bitcast_fusion.1 = f32[1,180,128]{2,1,0:T(8,128)S(1)} fusion(bf16[2048,128]{1,0:T(8,128)(2,1)S(1)} %bitcast.60, f32[2048,180]{0,1:T(8,128)} %get-tuple-element.46, f32[2048]{0:T(1024)S(1)} %div.59), kind=kOutput, calls=%fused_computation.49 | convolution fusion | flops 95109120 | bytes 2099200 | tf_op jit(solution)/shard_map/dot_general | solution.py:272
  93.6 0.5 fusion.31
  95.7 1.3 fusion.22
  97.0 13.2 %shard_map.150 = f32[256,128]{1,0:T(8,128)} custom-call(bf16[8,256,128]{2,1,0:T(8,128)(2,1)} %bitcast.63), custom_call_target="tpu_custom_call" | custom-call | tf_op jit(solution)/shard_map/pallas_call | solution.py:122
  110.2 1.0 multiply_reduce_fusion.3
  111.3 1.0 multiply_convert_fusion.13
  112.3 0.8 copy.19
  113.6 1.3 convolution_convert_fusion
  114.9 21.2 %shard_map.151 = (f32[8,96,128]{2,1,0:T(8,128)}, f32[8,128]{1,0:T(8,128)}) custom-call(bf16[8,96,128]{2,1,0:T(8,128)(2,1)} %bitcast.65, f32[8,128]{1,0:T(8,128)} %broadcast_in_dim.2.loss), custom_call_target="tpu_custom_call" | custom-call | tf_op jit(solution)/shard_map/pallas_call | solution.py:169
  136.1 1.2 slice.95
  137.9 1.8 %copy.21 = f32[768,128]{1,0:T(8,128)} copy(f32[768,128]{1,0:T(8,128)} %bitcast.64) | data formatting | bytes 786432
  (67 shorter events, 5.4 us)
Async XLA Ops:
  0.6 44.9 %copy-start = (bf16[768,128]{1,0:T(8,128)(2,1)S(1)}, bf16[768,128]{1,0:T(8,128)(2,1)}, u32[]{:S(2)}) copy-start(bf16[768,128]{1,0:T(8,128)(2,1)} %param.25) | copy-start | bytes 589828
  0.6 4.6 %copy-start.11 = (f32[768]{0:T(1024)S(1)}, f32[768]{0:T(1024)}, u32[]{:S(2)}) copy-start(f32[768]{0:T(1024)} %param.22) | copy-start | bytes 9220
  0.7 4.6 %copy-start.10 = (f32[3072]{0:T(1024)S(1)}, f32[3072]{0:T(1024)}, u32[]{:S(2)}) copy-start(f32[3072]{0:T(1024)} %param.20) | copy-start | bytes 36868
  44.3 0.7 copy-start.8
  44.3 0.7 copy-start.9
  45.5 1.2 copy-start.5
  46.7 29.9 %copy-start.7 = (f32[976]{0:T(1024)}, f32[976]{0:T(1024)S(1)}, u32[]{:S(2)}) copy-start(f32[976]{0:T(1024)S(1)} %add_rsqrt_fusion) | copy-start | bytes 11716
  68.3 6.6 %copy-start.1 = (bf16[8,256,128]{2,1,0:T(8,128)(2,1)S(1)}, bf16[8,256,128]{2,1,0:T(8,128)(2,1)}, u32[]{:S(2)}) copy-start(bf16[8,256,128]{2,1,0:T(8,128)(2,1)} %get-tuple-element.7) | copy-start | bytes 1572868
  89.1 3.7 %copy-start.2 = (f32[2048,180]{0,1:T(8,128)S(1)}, f32[2048,180]{0,1:T(8,128)}, u32[]{:S(2)}) copy-start(f32[2048,180]{0,1:T(8,128)} %get-tuple-element.44) | copy-start | bytes 4423684
  92.8 1.4 copy-start.4
  93.6 1.5 %copy-start.3 = (f32[2048,180]{0,1:T(8,128)S(1)}, f32[2048,180]{0,1:T(8,128)}, u32[]{:S(2)}) copy-start(f32[2048,180]{0,1:T(8,128)} %get-tuple-element.46) | copy-start | bytes 4423684
  95.6 15.6 %slice-start = ((f32[976]{0:T(1024)}), f32[256]{0:T(256)S(1)}, s32[]{:S(2)}) async-start(f32[976]{0:T(1024)} %copy-done.7), calls=%async_computation | async-start | bytes 2048 | tf_op jit(solution)/shard_map/slice | solution.py:282
  97.0 16.6 %copy-start.6 = (bf16[976,768]{1,0:T(8,128)(2,1)S(1)}, bf16[976,768]{1,0:T(8,128)(2,1)}, u32[]{:S(2)}) copy-start(bf16[976,768]{1,0:T(8,128)(2,1)} %copy-done.5) | copy-start | bytes 4497412
